TPU v7x, 32 devices: a whole 2x2x4 slice. The times are simulated.
32 devices in a mesh: frames: 4 (over x, core), feat: 8 (over z, y).
Axes of the slice: x: 2, y: 2, z: 4, core: 2. Of those that a mesh axis runs over, the one named last changes fastest.
Arguments:
- acoustic: float32 [1024, 440], P('frames'), may hold values from -6 to 6
- projection: float32 [440, 8192], P(None, 'feat'), may hold values from -0.25 to 0.25
- phases: float32 [8192], P('feat'), may hold values from -3.140625 to 3.140625
- labels: int32 [1024], P('frames'), may hold values from 0 to 146
- weights: float32 [147, 8192], P(None, 'feat'), may hold values from -1.5 to 1.5
- scaled_duals: float32 [147, 1024], P(None, 'frames'), may hold values from -7 to 7
Outputs:
- weights_out: float32 [147, 8192], P(None, 'feat')
- duals_out: float32 [147, 1024], P(None, ('frames', 'feat'))
- penalty: float32 [], replicated
All inputs are finite; a program needn't handle non-finite values.
Results may differ from a plain program's by a relative error of at most 0.0003.
Values sent between devices are 32-bit elements; how exact they have to be, the bound alone decides.
No kernel may reach another device: no remote copies, remote signals or barrier semaphores. Data moves between devices by JAX's collectives and lax.ppermute only.
A program may use at most 64 MiB of HBM per device.

v0:
```python
import jax
import jax.numpy as jnp
from jax import lax
from jax.sharding import PartitionSpec as P

ITERS = 2
highest = lax.Precision.HIGHEST
epsilon = 1e-06
ridge_weight = 2.0


def cosine_features(acoustic, projection, phases, total_features):
    mixed = (
        jnp.dot(acoustic, projection, precision=highest, preferred_element_type=jnp.float32)
        + phases[None, :]
    )
    return jnp.sqrt(2.0 / total_features) * jnp.cos(mixed)


def ridge_solve(factor, right):
    middle = lax.linalg.triangular_solve(
        factor, right, left_side=False, lower=True, transpose_a=True
    )
    return lax.linalg.triangular_solve(
        factor, middle, left_side=False, lower=True, transpose_a=False
    )


def proximal(predicted, duals, target, penalty):
    shifted = predicted + duals
    inner = (2.0 * target + penalty * shifted) / (2.0 + penalty)
    split = jnp.where(target * shifted < 1.0, inner, shifted)
    miss = predicted - split
    duals_next = duals + miss
    residual = split - duals_next - predicted
    return (miss, duals_next, residual)


def shards(acoustic, projection, phases, labels, weights, scaled_duals):
    frames_here = acoustic.shape[0]
    block_width = projection.shape[1]
    class_count = weights.shape[0]
    feat_count = lax.axis_size("feat")
    group_count = lax.axis_size("frames")
    total_features = block_width * feat_count
    total_frames = frames_here * group_count
    ridge = frames_here / total_features
    share = frames_here // feat_count
    offset = lax.axis_index("feat") * share
    basis = cosine_features(acoustic, projection, phases, total_features)
    inner_matrix = ridge * jnp.eye(frames_here, dtype=jnp.float32) + lax.dot_general(
        basis, basis, (((1,), (1,)), ((), ())), precision=highest
    )
    factor = jnp.linalg.cholesky(inner_matrix)
    classes = lax.broadcasted_iota(jnp.int32, (class_count, frames_here), 0)
    target = jnp.where(classes == labels[None, :], 1.0, -1.0).astype(jnp.float32)
    duals = scaled_duals
    penalty = jnp.ones((), jnp.float32)
    for iteration in range(ITERS):
        partial_value = lax.dot_general(weights, basis, (((1,), (1,)), ((), ())), precision=highest)
        predicted = lax.psum(partial_value, "feat")
        miss, duals, residual = proximal(predicted, duals, target, penalty)
        mine = lax.dynamic_slice_in_dim(miss, offset, share, 1)
        primal_part = jnp.sum(mine * mine)
        proj = (
            jnp.dot(residual, basis, precision=highest, preferred_element_type=jnp.float32)
            / feat_count
        )
        coef = lax.dot_general(proj, basis, (((1,), (1,)), ((), ())), precision=highest)
        solved = ridge_solve(factor, coef)
        back = jnp.dot(solved, basis, precision=highest, preferred_element_type=jnp.float32)
        local = weights + (proj - back) / ridge
        summed, primal_groups = lax.psum((local, primal_part), "frames")
        updated = penalty / (ridge_weight + penalty * group_count) * summed
        moved = updated - weights
        change, primal = lax.psum((jnp.sum(moved * moved), primal_groups), "feat")
        ratio = (primal / (total_frames * class_count) + epsilon) / (
            group_count * penalty * penalty * change / (total_features * class_count) + epsilon
        )
        next_penalty = penalty * jnp.sqrt(jnp.sqrt(ratio))
        duals = duals * (penalty / next_penalty)
        penalty = next_penalty
        weights = updated
    duals = lax.dynamic_slice_in_dim(duals, offset, share, 1)
    return (weights, duals, penalty)


def solution(mesh):
    return jax.shard_map(
        shards,
        mesh=mesh,
        in_specs=(
            P("frames", None),
            P(None, "feat"),
            P("feat"),
            P("frames"),
            P(None, "feat"),
            P(None, "frames"),
        ),
        out_specs=(P(None, "feat"), P(None, ("frames", "feat")), P()),
        check_vma=False,
    )
```

profile of v0, /device:TPU:0, one launch (start us, length us, event | category | flops | bytes accessed | tf_op | source)
XLA Modules:
  0.0 297.5 jit_solution(15187236382029461404)
XLA Ops:
  7.2 1.4 copy-done
  8.7 13.2 %fusion.1 = f32[256,1024]{1,0:T(8,128)S(1)} fusion(f32[256,440]{0,1:T(8,128)} %param.10, f32[440,1024]{1,0:T(8,128)S(1)} %copy-done, f32[1024]{0:T(1024)} %param.12), kind=kOutput, calls=%fused_computation.4 | convolution fusion | flops 1384644608 | bytes 3305472 | tf_op jit(solution)/shard_map/dot_general | solution.py:14
  21.8 1.9 convolution_bitcast_fusion
  24.0 1.7 fusion.69
  25.7 1.8 copy.9
  27.5 1.1 fusion.10
  28.6 0.7 copy-done.8
  29.3 0.6 cholesky.115
  29.9 12.5 %cholesky.49 = f32[128,128]{1,0:T(8,128)S(1)} custom-call(f32[128,128]{1,0:T(8,128)} %cholesky.115), custom_call_target="Cholesky" | custom-call | tf_op jit(solution)/shard_map/jit(cholesky)/cholesky | solution.py:54
  42.5 0.6 select_reduce_fusion.1
  43.1 11.3 %custom-call.17 = f32[1,128,128]{1,2,0:T(8,128)} custom-call(f32[1,128,128]{2,1,0:T(8,128)} %get-tuple-element.63), custom_call_target="InvertDiagBlocksLowerTriangular" | custom-call | tf_op jit(solution)/shard_map/jit(cholesky)/cholesky | solution.py:54
  54.4 0.7 cholesky.111
  55.1 1.7 constant_dynamic-update-slice_fusion
  56.8 1.7 convolution_subtract_fusion.6
  58.5 12.5 %cholesky.103 = f32[128,128]{1,0:T(8,128)S(1)} custom-call(f32[128,128]{1,0:T(8,128)} %convolution_subtract_fusion.6), custom_call_target="Cholesky" | custom-call | tf_op jit(solution)/shard_map/jit(cholesky)/cholesky | solution.py:54
  71.1 0.6 select_reduce_fusion
  71.7 0.7 compare_reduce_fusion
  73.8 1.7 select_select_fusion
  75.5 7.0 %while.8 = (s32[]{:T(128)}, f32[256,256]{1,0:T(8,128)}, s32[2,2]{1,0:T(2,128)S(1)}, f32[2,128,128]{2,1,0:T(8,128)}, s32[]{:T(128)}) while((s32[]{:T(128)}, f32[256,256]{1,0:T(8,128)}, s32[2,2]{1,0:T(2,128)S(1)}, f32[2,128,128]{2,1,0:T(8,128)}, s32[]{:T(128)}) %tuple.44), condition=%wide.while_cond, body=%wide.while_body.sunk | while | flops 2 | bytes 132205 | solution.py:21
  75.5 0.6 fusion.100
  76.1 2.9 bitcast_dynamic-update-slice_fusion.2
  79.1 0.6 fusion.100
  79.6 2.9 bitcast_dynamic-update-slice_fusion.2
  82.5 21.1 %custom-call.20 = f32[2,128,128]{1,2,0:T(8,128)} custom-call(f32[2,128,128]{2,1,0:T(8,128)} %get-tuple-element.33), custom_call_target="InvertDiagBlocksLowerTriangular" | custom-call | tf_op jit(solution)/shard_map/triangular_solve/custom-call.0 | solution.py:21
  103.6 1.7 fusion.66
  105.3 1.9 convolution_multiply_fusion.1
  107.2 1.2 fusion.70
  108.8 0.3 convolution_subtract_fusion.5
  110.2 1.6 fusion.3
  111.9 1.6 multiply_reduce_fusion.3
  113.5 9.0 %psum.71 = f32[]{:T(128)} all-reduce(f32[]{:T(128)} %multiply_reduce_fusion.3), channel_id=1, replica_groups=mesh['frames'=4,'feat'=8] {'frames'}, use_global_device_ids=true, to_apply=%region_2.3 | all-reduce | flops 1 | bytes 8 | tf_op jit(solution)/shard_map/psum | solution.py:73
  122.5 26.2 %all-reduce.10.cloned.1.call-done = f32[147,1024]{1,0:T(8,128)} async-done(((f32[147,1024]{1,0:T(8,128)}), f32[147,1024]{1,0:T(8,128)}) %all-reduce.10.cloned.1.call-update) | async-done | bytes 602128 | tf_op jit(solution)/shard_map/psum | solution.py:73
  148.7 3.0 %fusion.6 = f32[147,256]{1,0:T(8,128)} fusion(f32[256,1024]{1,0:T(8,128)S(1)} %fusion.1, f32[147,1024]{1,0:T(8,128)} %all-reduce.10.cloned.1.call-done), kind=kOutput, calls=%fused_computation.21 | convolution fusion | flops 462572544 | bytes 1801216 | tf_op jit(solution)/shard_map/dot_general | solution.py:60
  151.8 1.8 multiply_reduce_fusion.1
  153.6 22.0 %all-reduce.2 = (f32[]{:T(128)}, f32[]{:T(128)}) all-reduce(f32[]{:T(128)} %psum.71, f32[]{:T(128)} %multiply_reduce_fusion.1), channel_id=1, replica_groups=mesh['frames'=4,'feat'=8] {'feat'}, use_global_device_ids=true, to_apply=%region_3.4 | all-reduce | flops 2 | bytes 16 | tf_op jit(solution)/shard_map/psum | solution.py:76
  177.1 45.5 %all-reduce.12.cloned.1.call-done = f32[147,256]{1,0:T(8,128)} async-done(((f32[147,256]{1,0:T(8,128)}), f32[147,256]{1,0:T(8,128)}) %all-reduce.12.cloned.1.call-update) | async-done | bytes 150544 | tf_op jit(solution)/shard_map/psum | solution.py:61
  222.6 1.9 convolution_multiply_fusion
  224.4 1.2 fusion.71
  226.6 0.3 fusion.46
  227.1 0.3 fusion.43
  227.4 1.6 fusion.5
  229.1 1.1 fusion.54
  230.2 0.7 multiply_reduce_fusion.2
  230.9 6.3 %psum.77 = f32[]{:T(128)} all-reduce(f32[]{:T(128)} %multiply_reduce_fusion.2), channel_id=1, replica_groups=mesh['frames'=4,'feat'=8] {'frames'}, use_global_device_ids=true, to_apply=%region_14.17 | all-reduce | flops 1 | bytes 8 | tf_op jit(solution)/shard_map/psum | solution.py:73
  237.2 25.8 %all-reduce.14.cloned.1.call-done = f32[147,1024]{1,0:T(8,128)} async-done(((f32[147,1024]{1,0:T(8,128)}), f32[147,1024]{1,0:T(8,128)}) %all-reduce.14.cloned.1.call-update) | async-done | bytes 602128 | tf_op jit(solution)/shard_map/psum | solution.py:73
  263.0 2.6 multiply_reduce_fusion
  265.6 22.0 %all-reduce.1 = (f32[]{:T(128)}, f32[]{:T(128)}) all-reduce(f32[]{:T(128)} %psum.77, f32[]{:T(128)} %get-tuple-element.52), channel_id=1, replica_groups=mesh['frames'=4,'feat'=8] {'feat'}, use_global_device_ids=true, to_apply=%region_15.18 | all-reduce | flops 2 | bytes 16 | tf_op jit(solution)/shard_map/psum | solution.py:76
  289.2 0.7 copy.10
  (42 shorter events, 3.2 us)
Async XLA Ops:
  7.2 1.5 copy-start
  7.2 14.7 %copy-start.2 = (f32[147,1024]{1,0:T(8,128)S(1)}, f32[147,1024]{1,0:T(8,128)}, u32[]{:S(2)}) copy-start(f32[147,1024]{1,0:T(8,128)} %param.14) | copy-start | bytes 1806340
  7.2 96.4 %all-reduce.8.cloned.1.call-start = ((), (), s32[]{:S(2)}) async-start(), calls=%async_computation | async-start | bytes 311296 | tf_op jit(solution)/shard_map/psum | solution.py:61
  23.7 124.9 %all-reduce.10.cloned.1.call-start = ((), (), s32[]{:S(2)}) async-start(), calls=%async_computation.1 | async-start | bytes 1245184 | tf_op jit(solution)/shard_map/psum | solution.py:73
  27.5 76.1 %copy-start.9 = (s32[256]{0:T(256)S(1)}, s32[256]{0:T(256)}, u32[]{:S(2)}) copy-start(s32[256]{0:T(256)} %param.13) | copy-start | bytes 3076
  28.6 0.7 copy-start.8
  105.3 3.1 %copy-start.5 = (f32[147,256]{1,0:T(8,128)}, f32[147,256]{1,0:T(8,128)S(1)}, u32[]{:S(2)}) copy-start(f32[147,256]{1,0:T(8,128)S(1)} %get-tuple-element.54) | copy-start | bytes 451588
  105.3 3.1 %copy-start.6 = (f32[2,128,128]{1,2,0:T(8,128)S(1)}, f32[2,128,128]{1,2,0:T(8,128)}, u32[]{:S(2)}) copy-start(f32[2,128,128]{1,2,0:T(8,128)} %custom-call.20) | copy-start | bytes 393220
  105.3 3.4 %copy-start.3 = (f32[256,256]{1,0:T(8,128)S(1)}, f32[256,256]{1,0:T(8,128)}, u32[]{:S(2)}) copy-start(f32[256,256]{1,0:T(8,128)} %get-tuple-element.117) | copy-start | bytes 786436
  111.9 110.7 %all-reduce.12.cloned.1.call-start = ((), (), s32[]{:S(2)}) async-start(), calls=%async_computation.2 | async-start | bytes 311296 | tf_op jit(solution)/shard_map/psum | solution.py:61
  148.7 3.1 %copy-start.1 = (f32[147,1024]{1,0:T(8,128)S(1)}, f32[147,1024]{1,0:T(8,128)}, u32[]{:S(2)}) copy-start(f32[147,1024]{1,0:T(8,128)} %all-reduce.10.cloned.1.call-done) | copy-start | bytes 1806340
  151.7 111.3 %all-reduce.14.cloned.1.call-start = ((), (), s32[]{:S(2)}) async-start(), calls=%async_computation.3 | async-start | bytes 1245184 | tf_op jit(solution)/shard_map/psum | solution.py:73
  222.6 3.1 %copy-start.7 = (f32[2,128,128]{1,2,0:T(8,128)S(1)}, f32[2,128,128]{1,2,0:T(8,128)}, u32[]{:S(2)}) copy-start(f32[2,128,128]{1,2,0:T(8,128)} %custom-call.20) | copy-start | bytes 393220
  222.6 3.4 %copy-start.4 = (f32[256,256]{1,0:T(8,128)S(1)}, f32[256,256]{1,0:T(8,128)}, u32[]{:S(2)}) copy-start(f32[256,256]{1,0:T(8,128)} %get-tuple-element.117) | copy-start | bytes 786436
Sparse Core Ops, SparseCore 0:
  23.9 73.2 all-reduce.7
  112.0 36.6 all-reduce.9
  152.6 69.9 all-reduce.11
  229.2 33.7 all-reduce.13
where the time goes:
time: 299 us; the launch traced here: 298 us
  waiting for transfers between devices  97.5 us (33%)
  other arithmetic  71.9 us (24%)
  blocking collectives  59.2 us (20%)
  matrix products  36.1 us (12%)
  between operations  19.5 us (7%)
  local copies, waits for them, and re-layouts  13 us (4%)
    psum x2, waiting for transfers between devices, shards(): summed, primal_groups = lax.psum((local, primal_part), 'frames')  51.9 us
    psum x2, waiting for transfers between devices, shards(): predicted = lax.psum(partial_value, 'feat')  45.5 us
    psum x2, blocking collectives, shards(): change, primal = lax.psum((jnp.sum(moved * moved), primal_groups), 'feat')  44 us
    another operation x6, other arithmetic, shards(): factor = jnp.linalg.cholesky(inner_matrix)  38.4 us
    another operation x4, other arithmetic, ridge_solve(): lax.linalg.triangular_solve(factor, right, left_side=False, lower=True, t...  22.8 us
    psum x2, blocking collectives, shards(): summed, primal_groups = lax.psum((local, primal_part), 'frames')  15.3 us
    dot_general x1, matrix products, cosine_features(): jnp.dot(acoustic, projection, precision=highest, preferred_element_type=j...  13.2 us
    another operation x7, local copies, waits for them, and re-layouts, ridge_solve(): lax.linalg.triangular_solve(factor, right, left_side=False, lower=True, t...  7.03 us
  transfers between devices with their start and end apart: 4, of which 3 were waited for; matrix products, arithmetic and copies ran while one was open for 28% of the time, Pallas kernels for 0%

commit v1 on v0

--- a/solution.py
+++ b/solution.py
@@ -58,7 +58,11 @@
     penalty = jnp.ones((), jnp.float32)
     for iteration in range(ITERS):
         partial_value = lax.dot_general(weights, basis, (((1,), (1,)), ((), ())), precision=highest)
-        predicted = lax.psum(partial_value, "feat")
+        predicted = partial_value
+        for hop in (1, 2, 4):
+            predicted = predicted + lax.ppermute(
+                predicted, "feat", [(dev, dev ^ hop) for dev in range(8)]
+            )
         miss, duals, residual = proximal(predicted, duals, target, penalty)
         mine = lax.dynamic_slice_in_dim(miss, offset, share, 1)
         primal_part = jnp.sum(mine * mine)

time: 299 us -> 276 us (0.923)
  waiting for transfers between devices: 97.5 us -> 60.2 us
  starting transfers between devices: 0.34 us -> 12.7 us
  other arithmetic: 71.9 us -> 80.3 us
  blocking collectives: 59.2 us -> 53.9 us
    psum x2 -> x0, waiting for transfers between devices: 45.5 us -> none  [shards(): predicted = lax.psum(partial_value, 'feat')]
    ppermute x0 -> x6, starting transfers between devices: none -> 12.6 us  [shards(): lax.ppermute(predicted, 'feat', [(dev, dev ^ hop) for dev in range(8)])]
    ppermute x0 -> x6, waiting for transfers between devices: none -> 6.32 us  [shards(): lax.ppermute(predicted, 'feat', [(dev, dev ^ hop) for dev in range(8)])]
    add x0 -> x4, other arithmetic: none -> 5.69 us  [shards(): predicted + lax.ppermute(predicted, 'feat', [(dev, dev ^ hop) for dev in...]
  transfers between devices with their start and end apart: 4 -> 8, of which waited for: 3 -> 4; matrix products, arithmetic and copies ran while one was open for 28% -> 30% of each run, Pallas kernels for 0% -> 0%
where the time goes in v1:
time: 276 us; the launch traced here: 275 us
  other arithmetic  80.3 us (29%)
  waiting for transfers between devices  60.2 us (22%)
  blocking collectives  53.9 us (20%)
  matrix products  35.5 us (13%)
  between operations  19.7 us (7%)
  local copies, waits for them, and re-layouts  12.8 us (5%)
  starting transfers between devices  12.7 us (5%)
    psum x2, waiting for transfers between devices, shards(): summed, primal_groups = lax.psum((local, primal_part), 'frames')  53.8 us
    psum x2, blocking collectives, shards(): change, primal = lax.psum((jnp.sum(moved * moved), primal_groups), 'feat')  41.3 us
    another operation x6, other arithmetic, shards(): factor = jnp.linalg.cholesky(inner_matrix)  38.4 us
    another operation x4, other arithmetic, ridge_solve(): lax.linalg.triangular_solve(factor, right, left_side=False, lower=True, t...  22.8 us
    dot_general x1, matrix products, cosine_features(): jnp.dot(acoustic, projection, precision=highest, preferred_element_type=j...  13.3 us
    ppermute x6, starting transfers between devices, shards(): lax.ppermute(predicted, 'feat', [(dev, dev ^ hop) for dev in range(8)])  12.6 us
    psum x2, blocking collectives, shards(): summed, primal_groups = lax.psum((local, primal_part), 'frames')  12.6 us
    another operation x7, local copies, waits for them, and re-layouts, ridge_solve(): lax.linalg.triangular_solve(factor, right, left_side=False, lower=True, t...  6.82 us
  transfers between devices with their start and end apart: 8, of which 4 were waited for; matrix products, arithmetic and copies ran while one was open for 30% of the time, Pallas kernels for 0%

profile of v1, /device:TPU:0, one launch (start us, length us, event | category | flops | bytes accessed | tf_op | source)
XLA Modules:
  0.0 275.1 jit_solution(356546913883032916)
XLA Ops:
  7.2 1.4 copy-done
  8.7 13.3 %fusion.1 = f32[256,1024]{1,0:T(8,128)S(1)} fusion(f32[256,440]{0,1:T(8,128)} %param.10, f32[440,1024]{1,0:T(8,128)S(1)} %copy-done, f32[1024]{0:T(1024)} %param.12), kind=kOutput, calls=%fused_computation.4 | convolution fusion | flops 1384644608 | bytes 3305472 | tf_op jit(solution)/shard_map/dot_general | solution.py:14
  22.0 1.9 convolution_bitcast_fusion
  23.9 3.0 %collective-permute-start = (f32[147,256]{1,0:T(8,128)}, f32[147,256]{1,0:T(8,128)}, u32[]{:S(2)}, u32[]{:S(2)}) collective-permute-start(f32[147,256]{1,0:T(8,128)} %convolution_bitcast_fusion), channel_id=1, source_target_pairs={{0,1},{1,0},{2,3},{3,2},{4,5},{5,4},{6,7},{7,6},{8,9},{9,8},{10,11... | collective-permute-start | bytes 451592 | tf_op jit(solution)/shard_map/ppermute | solution.py:63
  26.9 1.7 fusion.69
  28.6 1.8 copy.9
  30.4 1.1 fusion.10
  32.8 12.5 %cholesky.49 = f32[128,128]{1,0:T(8,128)S(1)} custom-call(f32[128,128]{1,0:T(8,128)} %cholesky.115), custom_call_target="Cholesky" | custom-call | tf_op jit(solution)/shard_map/jit(cholesky)/cholesky | solution.py:54
  46.0 11.3 %custom-call.17 = f32[1,128,128]{1,2,0:T(8,128)} custom-call(f32[1,128,128]{2,1,0:T(8,128)} %get-tuple-element.64), custom_call_target="InvertDiagBlocksLowerTriangular" | custom-call | tf_op jit(solution)/shard_map/jit(cholesky)/cholesky | solution.py:54
  57.3 0.7 cholesky.111
  58.0 1.7 constant_dynamic-update-slice_fusion
  59.7 1.7 convolution_subtract_fusion.6
  61.4 12.7 %cholesky.103 = f32[128,128]{1,0:T(8,128)S(1)} custom-call(f32[128,128]{1,0:T(8,128)} %convolution_subtract_fusion.6), custom_call_target="Cholesky" | custom-call | tf_op jit(solution)/shard_map/jit(cholesky)/cholesky | solution.py:54
  76.7 1.7 add.119
  78.4 1.6 collective-permute-start.1
  79.9 1.7 select_select_fusion
  81.6 2.6 collective-permute-done.1
  84.2 1.7 add.120
  85.8 2.6 collective-permute-start.2
  88.5 6.8 %while.8 = (s32[]{:T(128)}, f32[256,256]{1,0:T(8,128)}, s32[2,2]{1,0:T(2,128)S(1)}, f32[2,128,128]{2,1,0:T(8,128)}, s32[]{:T(128)}) while((s32[]{:T(128)}, f32[256,256]{1,0:T(8,128)}, s32[2,2]{1,0:T(2,128)S(1)}, f32[2,128,128]{2,1,0:T(8,128)}, s32[]{:T(128)}) %tuple.45), condition=%wide.while_cond, body=%wide.while_body.sunk | while | flops 2 | bytes 132205 | solution.py:21
  89.1 2.8 %bitcast_dynamic-update-slice_fusion.2 = f32[2,128,128]{2,1,0:T(8,128)} fusion(f32[2,128,128]{2,1,0:T(8,128)} %get-tuple-element.106, s32[]{:T(128)S(6)} %copy.16, f32[256,256]{1,0:T(8,128)} %get-tuple-element.109, s32[]{:T(128)} %bitcast.83, s32[]{:T(128)} %bitcast.84), kind=kLoop, calls=%fused_computation.clone.1 | loop fusion | bytes 132100 | tf_op jit(solution)/shard_map/triangular_solve | solution.py:21
  92.5 2.8 %bitcast_dynamic-update-slice_fusion.2 = f32[2,128,128]{2,1,0:T(8,128)} fusion(f32[2,128,128]{2,1,0:T(8,128)} %get-tuple-element.106, s32[]{:T(128)S(6)} %copy.16, f32[256,256]{1,0:T(8,128)} %get-tuple-element.109, s32[]{:T(128)} %bitcast.83, s32[]{:T(128)} %bitcast.84), kind=kLoop, calls=%fused_computation.clone.1 | loop fusion | bytes 132100 | tf_op jit(solution)/shard_map/triangular_solve | solution.py:21
  95.3 21.1 %custom-call.20 = f32[2,128,128]{1,2,0:T(8,128)} custom-call(f32[2,128,128]{2,1,0:T(8,128)} %get-tuple-element.33), custom_call_target="InvertDiagBlocksLowerTriangular" | custom-call | tf_op jit(solution)/shard_map/triangular_solve/custom-call.0 | solution.py:21
  116.4 1.8 fusion.66
  118.2 1.8 convolution_multiply_fusion.1
  120.0 1.2 fusion.70
  123.0 1.6 fusion.3
  124.7 32.3 %all-reduce.6.cloned.1.call-done = f32[147,1024]{1,0:T(8,128)} async-done(((f32[147,1024]{1,0:T(8,128)}), f32[147,1024]{1,0:T(8,128)}) %all-reduce.6.cloned.1.call-update) | async-done | bytes 602128 | tf_op jit(solution)/shard_map/psum | solution.py:77
  157.0 2.4 fusion.6
  159.3 1.5 collective-permute-start.3
  160.9 3.8 %collective-permute-done.3 = f32[147,256]{1,0:T(8,128)S(1)} collective-permute-done((f32[147,256]{1,0:T(8,128)S(1)}, f32[147,256]{1,0:T(8,128)S(1)}, u32[]{:S(2)}, u32[]{:S(2)}) %collective-permute-start.3) | collective-permute-done | bytes 150560 | tf_op jit(solution)/shard_map/ppermute | solution.py:63
  165.3 1.5 collective-permute-start.4
  166.8 1.6 multiply_reduce_fusion.3
  168.4 6.3 %psum.56 = f32[]{:T(128)} all-reduce(f32[]{:T(128)} %multiply_reduce_fusion.3), channel_id=1, replica_groups=mesh['frames'=4,'feat'=8] {'frames'}, use_global_device_ids=true, to_apply=%region_1.2 | all-reduce | flops 1 | bytes 8 | tf_op jit(solution)/shard_map/psum | solution.py:77
  174.6 1.7 add.134
  176.3 2.4 collective-permute-start.5
  178.7 1.8 multiply_reduce_fusion.1
  180.6 19.3 %all-reduce.2 = (f32[]{:T(128)}, f32[]{:T(128)}) all-reduce(f32[]{:T(128)} %psum.56, f32[]{:T(128)} %multiply_reduce_fusion.1), channel_id=1, replica_groups=mesh['frames'=4,'feat'=8] {'feat'}, use_global_device_ids=true, to_apply=%region_2.3 | all-reduce | flops 2 | bytes 16 | tf_op jit(solution)/shard_map/psum | solution.py:80
  201.4 1.8 fusion.54
  203.2 1.8 convolution_multiply_fusion
  205.0 1.2 fusion.71
  208.0 1.6 fusion.5
  209.7 1.6 multiply_reduce_fusion.2
  211.3 6.3 %psum.61 = f32[]{:T(128)} all-reduce(f32[]{:T(128)} %multiply_reduce_fusion.2), channel_id=1, replica_groups=mesh['frames'=4,'feat'=8] {'frames'}, use_global_device_ids=true, to_apply=%region_12.15 | all-reduce | flops 1 | bytes 8 | tf_op jit(solution)/shard_map/psum | solution.py:77
  217.6 1.1 multiply_add_fusion
  218.7 21.5 %all-reduce.8.cloned.1.call-done = f32[147,1024]{1,0:T(8,128)} async-done(((f32[147,1024]{1,0:T(8,128)}), f32[147,1024]{1,0:T(8,128)}) %all-reduce.8.cloned.1.call-update) | async-done | bytes 602128 | tf_op jit(solution)/shard_map/psum | solution.py:77
  240.3 2.6 multiply_reduce_fusion
  242.9 22.0 %all-reduce.1 = (f32[]{:T(128)}, f32[]{:T(128)}) all-reduce(f32[]{:T(128)} %psum.61, f32[]{:T(128)} %get-tuple-element.52), channel_id=1, replica_groups=mesh['frames'=4,'feat'=8] {'feat'}, use_global_device_ids=true, to_apply=%region_13.16 | all-reduce | flops 2 | bytes 16 | tf_op jit(solution)/shard_map/psum | solution.py:80
  (55 shorter events, 9.6 us)
Async XLA Ops:
  7.2 1.5 copy-start
  7.2 14.8 %copy-start.2 = (f32[147,1024]{1,0:T(8,128)S(1)}, f32[147,1024]{1,0:T(8,128)}, u32[]{:S(2)}) copy-start(f32[147,1024]{1,0:T(8,128)} %param.14) | copy-start | bytes 1806340
  7.2 149.8 %all-reduce.6.cloned.1.call-start = ((), (), s32[]{:S(2)}) async-start(), calls=%async_computation | async-start | bytes 1245184 | tf_op jit(solution)/shard_map/psum | solution.py:77
  23.9 52.8 %collective-permute-start = (f32[147,256]{1,0:T(8,128)}, f32[147,256]{1,0:T(8,128)}, u32[]{:S(2)}, u32[]{:S(2)}) collective-permute-start(f32[147,256]{1,0:T(8,128)} %convolution_bitcast_fusion), channel_id=1, source_target_pairs={{0,1},{1,0},{2,3},{3,2},{4,5},{5,4},{6,7},{7,6},{8,9},{9,8},{10,11... | collective-permute-start | bytes 451592 | tf_op jit(solution)/shard_map/ppermute | solution.py:63
  31.5 0.7 copy-start.9
  32.2 84.2 %copy-start.10 = (s32[256]{0:T(256)S(1)}, s32[256]{0:T(256)}, u32[]{:S(2)}) copy-start(s32[256]{0:T(256)} %param.13) | copy-start | bytes 3076
  78.4 5.8 %collective-permute-start.1 = (f32[147,256]{1,0:T(8,128)}, f32[147,256]{1,0:T(8,128)}, u32[]{:S(2)}, u32[]{:S(2)}) collective-permute-start(f32[147,256]{1,0:T(8,128)} %add.119), channel_id=1, source_target_pairs={{0,2},{1,3},{2,0},{3,1},{4,6},{5,7},{6,4},{7,5},{8,10},{9,11},{10,... | collective-permute-start | bytes 451592 | tf_op jit(solution)/shard_map/ppermute | solution.py:63
  85.8 30.5 %collective-permute-start.2 = (f32[147,256]{1,0:T(8,128)}, f32[147,256]{1,0:T(8,128)}, u32[]{:S(2)}, u32[]{:S(2)}) collective-permute-start(f32[147,256]{1,0:T(8,128)} %add.120), channel_id=1, source_target_pairs={{0,4},{1,5},{2,6},{3,7},{4,0},{5,1},{6,2},{7,3},{8,12},{9,13},{10,... | collective-permute-start | bytes 451592 | tf_op jit(solution)/shard_map/ppermute | solution.py:63
  118.1 3.0 %copy-start.3 = (f32[147,256]{1,0:T(8,128)}, f32[147,256]{1,0:T(8,128)S(1)}, u32[]{:S(2)}) copy-start(f32[147,256]{1,0:T(8,128)S(1)} %get-tuple-element.56) | copy-start | bytes 451588
  118.2 3.0 %copy-start.6 = (f32[2,128,128]{1,2,0:T(8,128)S(1)}, f32[2,128,128]{1,2,0:T(8,128)}, u32[]{:S(2)}) copy-start(f32[2,128,128]{1,2,0:T(8,128)} %custom-call.20) | copy-start | bytes 393220
  118.2 3.3 %copy-start.4 = (f32[256,256]{1,0:T(8,128)S(1)}, f32[256,256]{1,0:T(8,128)}, u32[]{:S(2)}) copy-start(f32[256,256]{1,0:T(8,128)} %get-tuple-element.116) | copy-start | bytes 786436
  124.6 115.6 %all-reduce.8.cloned.1.call-start = ((), (), s32[]{:S(2)}) async-start(), calls=%async_computation.1 | async-start | bytes 1245184 | tf_op jit(solution)/shard_map/psum | solution.py:77
  157.0 21.8 %copy-start.1 = (f32[147,1024]{1,0:T(8,128)S(1)}, f32[147,1024]{1,0:T(8,128)}, u32[]{:S(2)}) copy-start(f32[147,1024]{1,0:T(8,128)} %all-reduce.6.cloned.1.call-done) | copy-start | bytes 1806340
  159.3 5.3 %collective-permute-start.3 = (f32[147,256]{1,0:T(8,128)S(1)}, f32[147,256]{1,0:T(8,128)S(1)}, u32[]{:S(2)}, u32[]{:S(2)}) collective-permute-start(f32[147,256]{1,0:T(8,128)S(1)} %fusion.6), channel_id=1, source_target_pairs={{0,1},{1,0},{2,3},{3,2},{4,5},{5,4},{6,7},{7,6},{8,9},{9,8},{10,11... | collective-permute-start | bytes 451592 | tf_op jit(solution)/shard_map/ppermute | solution.py:63
  165.3 9.3 %collective-permute-start.4 = (f32[147,256]{1,0:T(8,128)}, f32[147,256]{1,0:T(8,128)}, u32[]{:S(2)}, u32[]{:S(2)}) collective-permute-start(f32[147,256]{1,0:T(8,128)} %add.133), channel_id=1, source_target_pairs={{0,2},{1,3},{2,0},{3,1},{4,6},{5,7},{6,4},{7,5},{8,10},{9,11},{10,... | collective-permute-start | bytes 451592 | tf_op jit(solution)/shard_map/ppermute | solution.py:63
  176.3 25.0 %collective-permute-start.5 = (f32[147,256]{1,0:T(8,128)}, f32[147,256]{1,0:T(8,128)}, u32[]{:S(2)}, u32[]{:S(2)}) collective-permute-start(f32[147,256]{1,0:T(8,128)} %add.134), channel_id=1, source_target_pairs={{0,4},{1,5},{2,6},{3,7},{4,0},{5,1},{6,2},{7,3},{8,12},{9,13},{10,... | collective-permute-start | bytes 451592 | tf_op jit(solution)/shard_map/ppermute | solution.py:63
  203.2 3.1 %copy-start.8 = (f32[147,256]{1,0:T(8,128)}, f32[147,256]{1,0:T(8,128)S(1)}, u32[]{:S(2)}) copy-start(f32[147,256]{1,0:T(8,128)S(1)} %get-tuple-element.55) | copy-start | bytes 451588
  203.2 3.1 %copy-start.7 = (f32[2,128,128]{1,2,0:T(8,128)S(1)}, f32[2,128,128]{1,2,0:T(8,128)}, u32[]{:S(2)}) copy-start(f32[2,128,128]{1,2,0:T(8,128)} %custom-call.20) | copy-start | bytes 393220
  203.2 3.4 %copy-start.5 = (f32[256,256]{1,0:T(8,128)S(1)}, f32[256,256]{1,0:T(8,128)}, u32[]{:S(2)}) copy-start(f32[256,256]{1,0:T(8,128)} %get-tuple-element.116) | copy-start | bytes 786436
Sparse Core Ops, SparseCore 0:
  124.7 32.1 all-reduce.5
  209.8 30.3 all-reduce.7
